TPU v7x, 256 devices: a whole 4x4x8 slice. The times are simulated.
256 devices in a mesh: seq: 8 (over x, core), dp: 8 (over z), fsdp: 4 (over y).
Axes of the slice: x: 4, y: 4, z: 8, core: 2. Of those that a mesh axis runs over, the one named last changes fastest.
Arguments:
- query_rows: bfloat16 [32, 1024, 4096], P(('dp', 'fsdp'), 'seq'), may hold values from -2.5 to 2.5
- forward_key_rows: bfloat16 [32, 1024, 1024], P(('dp', 'fsdp'), 'seq'), may hold values from -2.5 to 2.5
- forward_value_rows: bfloat16 [32, 1024, 1024], P(('dp', 'fsdp'), 'seq'), may hold values from -4 to 4
- out_cotangent: bfloat16 [32, 1024, 4096], P(('dp', 'fsdp'), 'seq'), may hold values from -12 to 12
- proj_weight: bfloat16 [4096, 4096], P(('dp', 'fsdp'), 'seq'), may hold values from -0.09375 to 0.09375
- sent_lengths: int32 [32, 32], P(('dp', 'fsdp')), may hold values from 1 to 64, 1024 in all within a row
Outputs:
- query_grad: bfloat16 [32, 1024, 4096], P(('dp', 'fsdp'), 'seq')
- key_gradient: bfloat16 [32, 1024, 1024], P(('dp', 'fsdp'), 'seq')
- value_gradient: bfloat16 [32, 1024, 1024], P(('dp', 'fsdp'), 'seq')
- proj_grad: bfloat16 [4096, 4096], P(('dp', 'fsdp'), 'seq')
Inputs may be any that keep to these rules, and one draw needn't show every extreme that they name: `sent_lengths`: each window's 32 lengths sum to 1024, and the longest is exactly 64.
All inputs are finite; a program needn't handle non-finite values.
Results may differ from a plain program's by a relative error of at most 0.0058.
Values may be sent and summed in bfloat16 or wider, within the bound.
No kernel may reach another device: no remote copies, remote signals or barrier semaphores. Data moves between devices by JAX's collectives and lax.ppermute only.
A program may use at most 128 MiB of HBM per device.

v0:
```python
import math
import jax
import jax.numpy as jnp
from jax import lax
from jax.sharding import PartitionSpec as P

QUERY_HEADS = 32
KEY_VALUE_HEADS = 8
HEAD_SIZE = 128


def per_device(
    query_rows, forward_key_rows, forward_value_rows, out_cotangent, proj_weight, sent_lengths
):
    queries_per_group = QUERY_HEADS // KEY_VALUE_HEADS
    factor = 1.0 / math.sqrt(HEAD_SIZE)
    gathered = lax.all_gather(out_cotangent, "seq", axis=1, tiled=True)
    cotangent = gathered[0]
    length = cotangent.shape[0]
    sliced = cotangent
    upstream_gradient = jnp.dot(
        sliced,
        lax.all_gather(proj_weight, ("dp", "fsdp"), axis=0, tiled=True),
        preferred_element_type=jnp.float32,
    ).astype(jnp.bfloat16)
    heads_of_queries, heads_of_keys, heads_of_values = (
        lax.all_to_all(query_rows, "seq", split_axis=2, concat_axis=1, tiled=True),
        lax.all_to_all(forward_key_rows, "seq", split_axis=2, concat_axis=1, tiled=True),
        lax.all_to_all(forward_value_rows, "seq", split_axis=2, concat_axis=1, tiled=True),
    )
    heads_of_queries = heads_of_queries[0]
    heads_of_keys = heads_of_keys[0]
    heads_of_values = heads_of_values[0]
    bounds = jnp.cumsum(sent_lengths[0])
    places = jnp.arange(length, dtype=jnp.int32)
    sentence = jnp.sum((places[:, None] >= bounds[None, :]).astype(jnp.int32), axis=1)
    block_rows = min(512, length)
    block_count = length // block_rows
    group_cols = queries_per_group * HEAD_SIZE
    key_head = heads_of_keys
    value_head = heads_of_values
    query_group = heads_of_queries

    def block_step(block_index, buffers):
        output_buf, query_buf, key_buf, value_buf = buffers
        offset = block_index * block_rows
        query_block = lax.dynamic_slice_in_dim(query_group, offset, block_rows, 0).reshape(
            block_rows, queries_per_group, HEAD_SIZE
        )
        upstream_block = lax.dynamic_slice_in_dim(upstream_gradient, offset, block_rows, 0).reshape(
            block_rows, queries_per_group, HEAD_SIZE
        )
        sentence_query = lax.dynamic_slice_in_dim(sentence, offset, block_rows, 0)
        allowed = (sentence[None, :] <= sentence_query[:, None]) & (
            sentence[None, :] >= sentence_query[:, None] - 3
        )
        scores = (
            jnp.einsum("qhd,kd->hqk", query_block, key_head, preferred_element_type=jnp.float32)
            * factor
        )
        raised = jnp.where(allowed[None], jnp.exp(scores), 0.0)
        attend = raised / jnp.sum(raised, axis=-1, keepdims=True)
        rounded = attend.astype(jnp.bfloat16)
        output_block = jnp.einsum(
            "hqk,kd->qhd", rounded, value_head, preferred_element_type=jnp.float32
        ).astype(jnp.bfloat16)
        grad_attend = jnp.einsum(
            "qhd,kd->hqk", upstream_block, value_head, preferred_element_type=jnp.float32
        )
        dscore = (
            attend * (grad_attend - jnp.sum(attend * grad_attend, axis=-1, keepdims=True)) * factor
        ).astype(jnp.bfloat16)
        query_block_grad = jnp.einsum(
            "hqk,kd->qhd", dscore, key_head, preferred_element_type=jnp.float32
        ).astype(jnp.bfloat16)
        key_window_grad = jnp.einsum(
            "hqk,qhd->kd", dscore, query_block, preferred_element_type=jnp.float32
        )
        value_window_grad = jnp.einsum(
            "hqk,qhd->kd", rounded, upstream_block, preferred_element_type=jnp.float32
        )
        output_buf = lax.dynamic_update_slice_in_dim(
            output_buf, output_block.reshape(block_rows, group_cols), offset, 0
        )
        query_buf = lax.dynamic_update_slice_in_dim(
            query_buf, query_block_grad.reshape(block_rows, group_cols), offset, 0
        )
        key_old = key_buf
        key_buf = key_old + key_window_grad
        value_old = value_buf
        value_buf = value_old + value_window_grad
        return (output_buf, query_buf, key_buf, value_buf)

    starting = (
        jnp.zeros((length, group_cols), jnp.bfloat16),
        jnp.zeros((length, group_cols), jnp.bfloat16),
        jnp.zeros((length, HEAD_SIZE), jnp.float32),
        jnp.zeros((length, HEAD_SIZE), jnp.float32),
    )
    output_buf, query_buf, key_buf, value_buf = lax.fori_loop(0, block_count, block_step, starting)
    key_parts = key_buf.astype(jnp.bfloat16)
    value_parts = value_buf.astype(jnp.bfloat16)
    sliced = cotangent
    proj_grad = lax.psum_scatter(
        lax.dot_general(
            sliced, output_buf, (((0,), (0,)), ((), ())), preferred_element_type=jnp.float32
        ),
        ("dp", "fsdp"),
        scatter_dimension=0,
        tiled=True,
    ).astype(jnp.bfloat16)
    query_grad, key_gradient, value_gradient = (
        lax.all_to_all(query_buf[None], "seq", split_axis=1, concat_axis=2, tiled=True),
        lax.all_to_all(key_parts[None], "seq", split_axis=1, concat_axis=2, tiled=True),
        lax.all_to_all(value_parts[None], "seq", split_axis=1, concat_axis=2, tiled=True),
    )
    return (query_grad, key_gradient, value_gradient, proj_grad)


def solution(mesh):
    in_specs = (
        P(("dp", "fsdp"), "seq", None),
        P(("dp", "fsdp"), "seq", None),
        P(("dp", "fsdp"), "seq", None),
        P(("dp", "fsdp"), "seq", None),
        P(("dp", "fsdp"), "seq"),
        P(("dp", "fsdp"), None),
    )
    out_specs = (
        P(("dp", "fsdp"), "seq", None),
        P(("dp", "fsdp"), "seq", None),
        P(("dp", "fsdp"), "seq", None),
        P(("dp", "fsdp"), "seq"),
    )
    return jax.shard_map(
        per_device, mesh=mesh, in_specs=in_specs, out_specs=out_specs, check_vma=False
    )
```

profile of v0, /device:TPU:2, one launch (start us, length us, event | category | flops | bytes accessed | tf_op | source)
XLA Modules:
  0.0 523.4 jit_solution(18148174244381852680)
XLA Ops:
  8.7 1.3 copy.118
  10.5 2.2 reduce.2
  13.5 5.6 %all-to-all-start.1 = ((bf16[8,2,8192]{2,1,0:T(2,128)(2,1)}), bf16[8,2,8192]{2,1,0:T(2,128)(2,1)S(1)}, u32[]{:S(2)}, u32[]{:S(2)}) async-start(bf16[8,2,8192]{2,1,0:T(2,128)(2,1)} %reshape.146), calls=%async_computation.1 | async-start | bytes 524288 | tf_op jit(solution)/shard_map/all_to_all | solution.py:28
  19.1 1.3 copy.120
  20.4 2.2 reduce.3
  23.4 1.8 all-to-all-done.1
  25.2 5.4 %all-to-all-start.2 = ((bf16[8,2,8192]{2,1,0:T(2,128)(2,1)}), bf16[8,2,8192]{2,1,0:T(2,128)(2,1)}, u32[]{:S(2)}, u32[]{:S(2)}) async-start(bf16[8,2,8192]{2,1,0:T(2,128)(2,1)} %reshape.148), calls=%async_computation.2 | async-start | bytes 524288 | tf_op jit(solution)/shard_map/all_to_all | solution.py:29
  30.5 5.0 copy.116
  35.6 22.4 %reduce.1 = bf16[4096,128]{1,0:T(8,128)(2,1)S(1)} reduce(bf16[4096,1,128]{2,1,0:T(2,128)(2,1)S(1)} %bitcast.213, bf16[]{:T(256)} %broadcast.149), dimensions={1}, to_apply=%bitcast.128.reduce_sub_computation | reduce | bytes 2097154
  58.0 1.1 reshape.144
  59.1 4.8 all-to-all-start
  63.9 13.1 %reduce-scatter.2.cloned.1.call-start = ((), (), s32[]{:S(2)}) async-start(), calls=%async_computation.9 | async-start | bytes 8650752 | tf_op jit(solution)/shard_map/reduce_scatter | solution.py:104
  78.8 1.2 reshape.149
  81.2 1.1 copy.150
  82.4 1.5 copy.117
  83.9 11.5 %all-gather.5.cloned.1.call-done = bf16[4096,512]{1,0:T(8,128)(2,1)} async-done(((bf16[128,512]{1,0:T(8,128)(2,1)}), bf16[4096,512]{1,0:T(8,128)(2,1)}) %all-gather.5.cloned.1.call-update) | async-done | bytes 4194320 | tf_op jit(solution)/shard_map/all_gather | solution.py:23
  95.4 50.1 %all-gather.3.cloned.1.call-done = bf16[1,1024,4096]{2,1,0:T(8,128)(2,1)} async-done(((bf16[1,128,4096]{2,1,0:T(8,128)(2,1)}), bf16[1,1024,4096]{2,1,0:T(8,128)(2,1)}) %all-gather.3.cloned.1.call-update) | async-done | bytes 8388624 | tf_op jit(solution)/shard_map/all_gather | solution.py:17
  145.5 10.1 %fusion.40 = bf16[1024,512]{1,0:T(8,128)(2,1)} fusion(bf16[4096,512]{1,0:T(8,128)(2,1)} %all-gather.5.cloned.1.call-done, bf16[1,1024,4096]{2,1,0:T(8,128)(2,1)} %all-gather.3.cloned.1.call-done), kind=kOutput, calls=%fused_computation.43 | convolution fusion | flops 4295491584 | bytes 13631488 | tf_op jit(solution)/shard_map/dot_general | solution.py:21
  155.6 1.1 broadcast.95.clone
  157.8 112.1 %while.22 = (s32[]{:T(128)}, bf16[1024,512]{0,1:T(8,128)(2,1)}, bf16[1024,512]{0,1:T(8,128)(2,1)}, f32[1024,128]{1,0:T(8,128)}, f32[1024,128]{1,0:T(8,128)}, /*i...) while((s32[]{:T(128)}, bf16[1024,512]{0,1:T(8,128)(2,1)}, ...), condition=%wide.region_5.6_spmd.clone, body=%wide.region_2.5_spmd.clone.sunk | while | flops 3293057536 | bytes 138467776 | solution.py:100
  160.0 4.5 fusion.72
  164.5 2.3 bitcast_reduce_fusion.2
  166.7 3.2 copy-done.11
  170.0 2.5 fusion.76
  172.5 17.1 %fusion.75 = f32[1024,128]{1,0:T(8,128)} fusion(bf16[512,4,128]{0,2,1:T(8,128)(2,1)S(1)} %bitcast.207, f32[512,4,1024]{2,0,1:T(8,128)} %fusion.72, f32[1024,128]{1,0:T(8,128)} %get-tuple-element.478, pred[]{:T(512)S(6)} %compare.3, f32[512,4,1024]{2,0,1:T(8,128)} %copy-done.11, f32[4,512]{1,0:T(4,128)S(1)} %get-tuple-element.458, ...), kind=kOutput, calls=%fused_computation.21.clone.1 | convolution fusion | flops 560204800 | bytes 18882560 | tf_op jit(solution)/shard_map/while/body/eval_jaxpr/hqk,qhd->kd/dot_general | solution.py:76
  189.6 16.9 %fusion.73 = bf16[4,512,128]{1,2,0:T(8,128)(2,1)S(1)} fusion(f32[512,4,1024]{2,0,1:T(8,128)} %fusion.72, bf16[1024,128]{0,1:T(8,128)(2,1)} %get-tuple-element.496, f32[512,4,1024]{2,0,1:T(8,128)} %copy-done.11, f32[4,512]{1,0:T(4,128)S(1)} %get-tuple-element.458, pred[512,1024]{1,0:T(8,128)(4,1)S(1)} %compare_and_fusion.2), kind=kOutput, calls=%fused_computation.18.clone.1 | convolution fusion | flops 560204800 | bytes 18096128 | tf_op jit(solution)/shard_map/while/body/eval_jaxpr/hqk,kd->qhd/dot_general | solution.py:73
  206.5 5.8 %fusion.74 = bf16[4,512,128]{1,2,0:T(8,128)(2,1)S(1)} fusion(bf16[1024,128]{1,0:T(8,128)(2,1)S(1)} %get-tuple-element.497, f32[512,4,1024]{2,0,1:T(8,128)} %copy-done.11, f32[4,512]{1,0:T(4,128)S(1)} %get-tuple-element.458, pred[512,1024]{1,0:T(8,128)(4,1)S(1)} %compare_and_fusion.2), kind=kOutput, calls=%fused_computation.17.clone.1 | convolution fusion | flops 545521664 | bytes 9707520 | tf_op jit(solution)/shard_map/while/body/eval_jaxpr/hqk,kd->qhd/dot_general | solution.py:64
  216.0 4.5 fusion.72
  220.5 2.3 bitcast_reduce_fusion.2
  222.8 3.2 copy-done.11
  226.0 2.5 fusion.76
  228.5 17.1 %fusion.75 = f32[1024,128]{1,0:T(8,128)} fusion(bf16[512,4,128]{0,2,1:T(8,128)(2,1)S(1)} %bitcast.207, f32[512,4,1024]{2,0,1:T(8,128)} %fusion.72, f32[1024,128]{1,0:T(8,128)} %get-tuple-element.478, pred[]{:T(512)S(6)} %compare.3, f32[512,4,1024]{2,0,1:T(8,128)} %copy-done.11, f32[4,512]{1,0:T(4,128)S(1)} %get-tuple-element.458, ...), kind=kOutput, calls=%fused_computation.21.clone.1 | convolution fusion | flops 560204800 | bytes 18882560 | tf_op jit(solution)/shard_map/while/body/eval_jaxpr/hqk,qhd->kd/dot_general | solution.py:76
  245.6 16.9 %fusion.73 = bf16[4,512,128]{1,2,0:T(8,128)(2,1)S(1)} fusion(f32[512,4,1024]{2,0,1:T(8,128)} %fusion.72, bf16[1024,128]{0,1:T(8,128)(2,1)} %get-tuple-element.496, f32[512,4,1024]{2,0,1:T(8,128)} %copy-done.11, f32[4,512]{1,0:T(4,128)S(1)} %get-tuple-element.458, pred[512,1024]{1,0:T(8,128)(4,1)S(1)} %compare_and_fusion.2), kind=kOutput, calls=%fused_computation.18.clone.1 | convolution fusion | flops 560204800 | bytes 18096128 | tf_op jit(solution)/shard_map/while/body/eval_jaxpr/hqk,kd->qhd/dot_general | solution.py:73
  262.6 5.8 %fusion.74 = bf16[4,512,128]{1,2,0:T(8,128)(2,1)S(1)} fusion(bf16[1024,128]{1,0:T(8,128)(2,1)S(1)} %get-tuple-element.497, f32[512,4,1024]{2,0,1:T(8,128)} %copy-done.11, f32[4,512]{1,0:T(4,128)S(1)} %get-tuple-element.458, pred[512,1024]{1,0:T(8,128)(4,1)S(1)} %compare_and_fusion.2), kind=kOutput, calls=%fused_computation.17.clone.1 | convolution fusion | flops 545521664 | bytes 9707520 | tf_op jit(solution)/shard_map/while/body/eval_jaxpr/hqk,kd->qhd/dot_general | solution.py:64
  269.9 11.4 %fusion.37 = f32[4096,512]{0,1:T(8,128)} fusion(bf16[1024,512]{0,1:T(8,128)(2,1)} %get-tuple-element.252, bf16[1,1024,4096]{2,1,0:T(8,128)(2,1)} %all-gather.3.cloned.1.call-done), kind=kOutput, calls=%fused_computation.42 | convolution fusion | flops 4294967296 | bytes 17825792 | tf_op jit(solution)/shard_map/dot_general | solution.py:105
  283.0 2.2 reduce.6
  286.0 4.7 all-to-all-start.5
  291.1 2.2 reduce.5
  294.1 2.7 all-to-all-done.5
  296.8 5.6 %all-to-all-start.4 = ((bf16[8,2,8192]{2,1,0:T(2,128)(2,1)}), bf16[8,2,8192]{2,1,0:T(2,128)(2,1)}, u32[]{:S(2)}, u32[]{:S(2)}) async-start(bf16[8,2,8192]{2,1,0:T(2,128)(2,1)} %reshape.152), calls=%async_computation.4 | async-start | bytes 524288 | tf_op jit(solution)/shard_map/all_to_all | solution.py:114
  302.4 1.8 copy.126
  304.3 7.1 %reduce.4 = bf16[1024,512]{1,0:T(8,128)(2,1)S(1)} reduce(bf16[1024,1,512]{2,1,0:T(2,128)(2,1)S(1)} %bitcast.212, bf16[]{:T(256)} %broadcast.149), dimensions={1}, to_apply=%bitcast.134.reduce_sub_computation | reduce | bytes 2097154
  311.3 1.6 reshape.150
  312.9 4.8 all-to-all-start.3
  319.1 1.2 reshape.153
  321.4 10.9 %all-to-all-done.3 = bf16[8,2,32768]{2,1,0:T(2,128)(2,1)S(1)} async-done(((bf16[8,2,32768]{2,1,0:T(2,128)(2,1)}), bf16[8,2,32768]{2,1,0:T(2,128)(2,1)S(1)}, u32[]{:S(2)}, u32[]{:S(2)}) %all-to-all-start.3) | async-done | bytes 1048608 | tf_op jit(solution)/shard_map/all_to_all | solution.py:113
  334.2 1.3 copy.132
  335.5 179.4 %reduce-scatter.2.cloned.1.call-done = f32[128,512]{0,1:T(8,128)} async-done(((f32[4096,512]{0,1:T(8,128)}), f32[128,512]{0,1:T(8,128)}) %reduce-scatter.2.cloned.1.call-update) | async-done | bytes 262160 | tf_op jit(solution)/shard_map/reduce_scatter | solution.py:104
  (94 shorter events, 24.6 us)
Async XLA Ops:
  7.2 88.2 %all-gather.5.cloned.1.call-start = ((), (), s32[]{:S(2)}) async-start(), calls=%async_computation.8 | async-start | bytes 4325376 | tf_op jit(solution)/shard_map/all_gather | solution.py:23
  7.9 69.1 %copy-start.10 = (s32[1,32]{1,0:T(1,128)S(1)}, s32[1,32]{1,0:T(1,128)}, u32[]{:S(2)}) copy-start(s32[1,32]{1,0:T(1,128)} %param.13) | copy-start | bytes 388
  7.9 137.6 %all-gather.3.cloned.1.call-start = ((), (), s32[]{:S(2)}) async-start(), calls=%async_computation.7 | async-start | bytes 9437184 | tf_op jit(solution)/shard_map/all_gather | solution.py:17
  13.5 11.6 %all-to-all-start.1 = ((bf16[8,2,8192]{2,1,0:T(2,128)(2,1)}), bf16[8,2,8192]{2,1,0:T(2,128)(2,1)S(1)}, u32[]{:S(2)}, u32[]{:S(2)}) async-start(bf16[8,2,8192]{2,1,0:T(2,128)(2,1)} %reshape.146), calls=%async_computation.1 | async-start | bytes 524288 | tf_op jit(solution)/shard_map/all_to_all | solution.py:28
  25.2 33.9 %all-to-all-start.2 = ((bf16[8,2,8192]{2,1,0:T(2,128)(2,1)}), bf16[8,2,8192]{2,1,0:T(2,128)(2,1)}, u32[]{:S(2)}, u32[]{:S(2)}) async-start(bf16[8,2,8192]{2,1,0:T(2,128)(2,1)} %reshape.148), calls=%async_computation.2 | async-start | bytes 524288 | tf_op jit(solution)/shard_map/all_to_all | solution.py:29
  59.1 21.1 %all-to-all-start = ((bf16[8,2,32768]{2,1,0:T(2,128)(2,1)}), bf16[8,2,32768]{2,1,0:T(2,128)(2,1)S(1)}, u32[]{:S(2)}, u32[]{:S(2)}) async-start(bf16[8,2,32768]{2,1,0:T(2,128)(2,1)} %reshape.144), calls=%async_computation | async-start | bytes 2097152 | tf_op jit(solution)/shard_map/all_to_all | solution.py:27
  63.9 451.0 %reduce-scatter.2.cloned.1.call-start = ((), (), s32[]{:S(2)}) async-start(), calls=%async_computation.9 | async-start | bytes 8650752 | tf_op jit(solution)/shard_map/reduce_scatter | solution.py:104
  159.9 4.5 copy-start.9
  159.9 10.0 %copy-start.5 = (f32[1024,128]{1,0:T(8,128)S(1)}, f32[1024,128]{1,0:T(8,128)}, u32[]{:S(2)}) copy-start(f32[1024,128]{1,0:T(8,128)} %get-tuple-element.479) | copy-start | bytes 1572868 | tf_op jit(solution)/shard_map/while
  166.7 3.2 copy-start.11
  172.5 17.1 %copy-start.6 = (f32[1024,128]{1,0:T(8,128)}, f32[1024,128]{1,0:T(8,128)S(1)}, u32[]{:S(2)}) copy-start(f32[1024,128]{1,0:T(8,128)S(1)} %fusion.76) | copy-start | bytes 1572868 | tf_op jit(solution)/shard_map/while
  206.5 5.8 %copy-start = (bf16[1024,512]{0,1:T(8,128)(2,1)S(1)}, bf16[1024,512]{0,1:T(8,128)(2,1)}, u32[]{:S(2)}) copy-start(bf16[1024,512]{0,1:T(8,128)(2,1)} %get-tuple-element.477) | copy-start | bytes 3145732 | tf_op jit(solution)/shard_map/while
  206.5 5.8 %copy-start.3 = (bf16[1024,512]{0,1:T(8,128)(2,1)S(1)}, bf16[1024,512]{0,1:T(8,128)(2,1)}, u32[]{:S(2)}) copy-start(bf16[1024,512]{0,1:T(8,128)(2,1)} %get-tuple-element.476) | copy-start | bytes 3145732 | tf_op jit(solution)/shard_map/while
  212.5 1.0 copy-start.1
  212.5 1.3 copy-start.4
  216.0 4.5 copy-start.9
  216.0 10.0 %copy-start.5 = (f32[1024,128]{1,0:T(8,128)S(1)}, f32[1024,128]{1,0:T(8,128)}, u32[]{:S(2)}) copy-start(f32[1024,128]{1,0:T(8,128)} %get-tuple-element.479) | copy-start | bytes 1572868 | tf_op jit(solution)/shard_map/while
  222.8 3.2 copy-start.11
  228.5 17.1 %copy-start.6 = (f32[1024,128]{1,0:T(8,128)}, f32[1024,128]{1,0:T(8,128)S(1)}, u32[]{:S(2)}) copy-start(f32[1024,128]{1,0:T(8,128)S(1)} %fusion.76) | copy-start | bytes 1572868 | tf_op jit(solution)/shard_map/while
  262.6 5.8 %copy-start = (bf16[1024,512]{0,1:T(8,128)(2,1)S(1)}, bf16[1024,512]{0,1:T(8,128)(2,1)}, u32[]{:S(2)}) copy-start(bf16[1024,512]{0,1:T(8,128)(2,1)} %get-tuple-element.477) | copy-start | bytes 3145732 | tf_op jit(solution)/shard_map/while
  262.6 5.8 %copy-start.3 = (bf16[1024,512]{0,1:T(8,128)(2,1)S(1)}, bf16[1024,512]{0,1:T(8,128)(2,1)}, u32[]{:S(2)}) copy-start(bf16[1024,512]{0,1:T(8,128)(2,1)} %get-tuple-element.476) | copy-start | bytes 3145732 | tf_op jit(solution)/shard_map/while
  268.6 1.0 copy-start.1
  268.6 1.3 copy-start.4
  281.3 1.0 copy-start.7
  281.3 1.2 copy-start.8
  281.3 21.1 %copy-start.2 = (bf16[1024,512]{0,1:T(8,128)(2,1)S(1)}, bf16[1024,512]{0,1:T(8,128)(2,1)}, u32[]{:S(2)}) copy-start(bf16[1024,512]{0,1:T(8,128)(2,1)} %get-tuple-element.249) | copy-start | bytes 3145732
  286.0 10.7 %all-to-all-start.5 = ((bf16[8,2,8192]{2,1,0:T(2,128)(2,1)}), bf16[8,2,8192]{2,1,0:T(2,128)(2,1)S(1)}, u32[]{:S(2)}, u32[]{:S(2)}) async-start(bf16[8,2,8192]{2,1,0:T(2,128)(2,1)} %reshape.154), calls=%async_computation.5 | async-start | bytes 524288 | tf_op jit(solution)/shard_map/all_to_all | solution.py:115
  296.8 16.2 %all-to-all-start.4 = ((bf16[8,2,8192]{2,1,0:T(2,128)(2,1)}), bf16[8,2,8192]{2,1,0:T(2,128)(2,1)}, u32[]{:S(2)}, u32[]{:S(2)}) async-start(bf16[8,2,8192]{2,1,0:T(2,128)(2,1)} %reshape.152), calls=%async_computation.4 | async-start | bytes 524288 | tf_op jit(solution)/shard_map/all_to_all | solution.py:114
  312.9 19.3 %all-to-all-start.3 = ((bf16[8,2,32768]{2,1,0:T(2,128)(2,1)}), bf16[8,2,32768]{2,1,0:T(2,128)(2,1)S(1)}, u32[]{:S(2)}, u32[]{:S(2)}) async-start(bf16[8,2,32768]{2,1,0:T(2,128)(2,1)} %reshape.150), calls=%async_computation.3 | async-start | bytes 2097152 | tf_op jit(solution)/shard_map/all_to_all | solution.py:113
Sparse Core Ops, SparseCore 0:
  10.6 84.7 all-gather.4
  97.2 48.1 all-gather.2
  281.5 233.3 reduce-scatter.1
where the time goes:
time: 531 us; the launch traced here: 523 us
  waiting for transfers between devices  258 us (49%)
  matrix products  120 us (23%)
  local copies, waits for them, and re-layouts  46.6 us (9%)
  starting transfers between devices  44 us (8%)
  other arithmetic  40.9 us (8%)
  between operations  14.3 us (3%)
    reduce_scatter x1, waiting for transfers between devices, per_device(): lax.psum_scatter(lax.dot_general(sliced, output_buf, (((0,), (0,)), ((),...  179 us
    all_gather x1, waiting for transfers between devices, per_device(): gathered = lax.all_gather(out_cotangent, 'seq', axis=1, tiled=True)  50.1 us
    unnamed x8, other arithmetic  38.5 us
    dot_general x2, matrix products, block_step(): jnp.einsum('hqk,qhd->kd', dscore, query_block, preferred_element_type=jnp...  34.2 us
    dot_general x2, matrix products, block_step(): jnp.einsum('hqk,kd->qhd', dscore, key_head, preferred_element_type=jnp.fl...  33.9 us
    unnamed x35, local copies, waits for them, and re-layouts  26.2 us
    reduce_scatter x1, starting transfers between devices, per_device(): lax.psum_scatter(lax.dot_general(sliced, output_buf, (((0,), (0,)), ((),...  13.1 us
    dot_general x2, matrix products, block_step(): jnp.einsum('hqk,kd->qhd', rounded, value_head, preferred_element_type=jnp...  11.5 us
  transfers between devices with their start and end apart: 9, of which 6 were waited for; matrix products, arithmetic and copies ran while one was open for 13% of the time, Pallas kernels for 0%

commit v1 on v0

--- a/solution.py
+++ b/solution.py
@@ -14,7 +14,8 @@
 ):
     queries_per_group = QUERY_HEADS // KEY_VALUE_HEADS
     factor = 1.0 / math.sqrt(HEAD_SIZE)
-    gathered = lax.all_gather(out_cotangent, "seq", axis=1, tiled=True)
+    sent = jnp.stack([out_cotangent] * lax.axis_size("seq"))
+    gathered = jnp.concatenate(lax.all_to_all(sent, "seq", 0, 0), axis=1)
     cotangent = gathered[0]
     length = cotangent.shape[0]
     sliced = cotangent

time: 531 us -> 571 us (1.075)
  waiting for transfers between devices: 258 us -> 282 us
  local copies, waits for them, and re-layouts: 46.6 us -> 53.4 us
  starting transfers between devices: 44 us -> 50.5 us
    all_to_all x0 -> x1, waiting for transfers between devices: none -> 73.4 us  [per_device(): gathered = jnp.concatenate(lax.all_to_all(sent, 'seq', 0, 0), axis=1)]
    all_gather x1 -> x0, waiting for transfers between devices: 50.1 us -> none  [per_device(): gathered = lax.all_gather(out_cotangent, 'seq', axis=1, tiled=True)]
    all_to_all x1, waiting for transfers between devices: 0.01 us -> 13.8 us  [per_device(): lax.all_to_all(query_rows, 'seq', split_axis=2, concat_axis=1, tiled=True)]
    all_gather x1, waiting for transfers between devices: 11.5 us -> 0.01 us  [per_device(): lax.all_gather(proj_weight, ('dp', 'fsdp'), axis=0, tiled=True)]
    all_to_all x0 -> x1, starting transfers between devices: none -> 6.44 us  [per_device(): gathered = jnp.concatenate(lax.all_to_all(sent, 'seq', 0, 0), axis=1)]
    unnamed x35 -> x33, local copies, waits for them, and re-layouts: 26.2 us -> 26.1 us
  transfers between devices with their start and end apart: 9 -> 9, of which waited for: 6 -> 6; matrix products, arithmetic and copies ran while one was open for 13% -> 12% of each run, Pallas kernels for 0% -> 0%
where the time goes in v1:
time: 571 us; the launch traced here: 563 us
  waiting for transfers between devices  282 us (49%)
  matrix products  120 us (21%)
  local copies, waits for them, and re-layouts  53.4 us (9%)
  starting transfers between devices  50.5 us (9%)
  other arithmetic  41.9 us (7%)
  between operations  14.5 us (3%)
    reduce_scatter x1, waiting for transfers between devices, per_device(): lax.psum_scatter(lax.dot_general(sliced, output_buf, (((0,), (0,)), ((),...  179 us
    all_to_all x1, waiting for transfers between devices, per_device(): gathered = jnp.concatenate(lax.all_to_all(sent, 'seq', 0, 0), axis=1)  73.4 us
    unnamed x8, other arithmetic  38.5 us
    dot_general x2, matrix products, block_step(): jnp.einsum('hqk,kd->qhd', dscore, key_head, preferred_element_type=jnp.fl...  33.8 us
    dot_general x2, matrix products, block_step(): jnp.einsum('hqk,qhd->kd', dscore, query_block, preferred_element_type=jnp...  32.2 us
    unnamed x33, local copies, waits for them, and re-layouts  26.1 us
    all_to_all x1, waiting for transfers between devices, per_device(): lax.all_to_all(query_rows, 'seq', split_axis=2, concat_axis=1, tiled=True)  13.8 us
    reduce_scatter x1, starting transfers between devices, per_device(): lax.psum_scatter(lax.dot_general(sliced, output_buf, (((0,), (0,)), ((),...  13 us
  transfers between devices with their start and end apart: 9, of which 6 were waited for; matrix products, arithmetic and copies ran while one was open for 12% of the time, Pallas kernels for 0%

profile of v1, /device:TPU:2, one launch (start us, length us, event | category | flops | bytes accessed | tf_op | source)
XLA Modules:
  0.0 562.7 jit_solution(15571753905118896288)
XLA Ops:
  7.2 1.3 copy.118
  9.0 2.2 reduce.2
  12.0 5.6 all-to-all-start.1
  17.6 1.3 copy.120
  18.9 2.2 reduce.3
  21.9 1.8 all-to-all-done.1
  23.7 5.4 all-to-all-start.2
  29.0 5.0 copy.116
  34.1 22.4 %reduce.1 = bf16[4096,128]{1,0:T(8,128)(2,1)S(1)} reduce(bf16[4096,1,128]{2,1,0:T(2,128)(2,1)S(1)} %bitcast.208, bf16[]{:T(256)} %broadcast.152), dimensions={1}, to_apply=%bitcast.121.reduce_sub_computation | reduce | bytes 2097154
  57.6 4.8 all-to-all-start
  63.2 13.8 %all-to-all-done = bf16[8,2,32768]{2,1,0:T(2,128)(2,1)S(1)} async-done(((bf16[8,2,32768]{2,1,0:T(2,128)(2,1)}), bf16[8,2,32768]{2,1,0:T(2,128)(2,1)S(1)}, u32[]{:S(2)}, u32[]{:S(2)}) %all-to-all-start) | async-done | bytes 1048608 | tf_op jit(solution)/shard_map/all_to_all | solution.py:28
  76.9 5.5 stack.2
  82.4 6.4 %all-to-all-start.3 = ((bf16[8,1,128,4096]{3,2,1,0:T(8,128)(2,1)}), bf16[8,1,128,4096]{3,2,1,0:T(8,128)(2,1)}, u32[]{:S(2)}, u32[]{:S(2)}) async-start(bf16[8,1,128,4096]{3,2,1,0:T(8,128)(2,1)} %stack.2), calls=%async_computation.3 | async-start | bytes 16777216 | tf_op jit(solution)/shard_map/all_to_all | solution.py:18
  88.8 13.0 %reduce-scatter.2.cloned.1.call-start = ((), (), s32[]{:S(2)}) async-start(), calls=%async_computation.9 | async-start | bytes 8650752 | tf_op jit(solution)/shard_map/reduce_scatter | solution.py:105
  103.6 1.2 reshape.152
  107.2 1.5 copy.117
  108.7 73.4 %all-to-all-done.3 = bf16[8,1,128,4096]{3,2,1,0:T(8,128)(2,1)} async-done(((bf16[8,1,128,4096]{3,2,1,0:T(8,128)(2,1)}), bf16[8,1,128,4096]{3,2,1,0:T(8,128)(2,1)}, u32[]{:S(2)}, u32[]{:S(2)}) %all-to-all-start.3) | async-done | bytes 8388640 | tf_op jit(solution)/shard_map/all_to_all | solution.py:18
  182.1 10.1 %convolution_convert_fusion = bf16[1024,512]{1,0:T(8,128)(2,1)} fusion(bf16[1024,4096]{1,0:T(8,128)(2,1)} %bitcast.8, bf16[4096,512]{1,0:T(8,128)(2,1)} %all-gather.2.cloned.1.call-done), kind=kOutput, calls=%fused_computation.39 | convolution fusion | flops 4295491584 | bytes 13631488 | tf_op jit(solution)/shard_map/dot_general | solution.py:22
  194.4 114.3 %while.22 = (s32[]{:T(128)}, bf16[1024,512]{0,1:T(8,128)(2,1)}, bf16[1024,512]{0,1:T(8,128)(2,1)}, f32[1024,128]{1,0:T(8,128)}, f32[1024,128]{1,0:T(8,128)}, /*i...) while((s32[]{:T(128)}, bf16[1024,512]{0,1:T(8,128)(2,1)}, ...), condition=%wide.region_5.6_spmd.clone, body=%wide.region_2.5_spmd.clone.sunk | while | flops 3293057536 | bytes 138467776 | solution.py:101
  196.6 4.5 fusion.64
  201.1 2.3 bitcast_reduce_fusion.2
  203.3 3.2 copy-done.10
  206.6 3.3 fusion.68
  209.8 16.1 %fusion.67 = f32[1024,128]{1,0:T(8,128)S(1)} fusion(bf16[512,4,128]{0,2,1:T(8,128)(2,1)S(1)} %bitcast.202, f32[512,4,1024]{2,0,1:T(8,128)} %fusion.64, f32[1024,128]{1,0:T(8,128)S(1)} %copy-done.5, pred[]{:T(512)S(6)} %compare.3, f32[512,4,1024]{2,0,1:T(8,128)} %copy-done.10, f32[4,512]{1,0:T(4,128)S(1)} %get-tuple-element.458, ...), kind=kOutput, calls=%fused_computation.21.clone.1 | convolution fusion | flops 560204800 | bytes 18882560 | tf_op jit(solution)/shard_map/while/body/eval_jaxpr/hqk,qhd->kd/dot_general | solution.py:77
  226.8 16.9 %fusion.65 = bf16[4,512,128]{1,2,0:T(8,128)(2,1)S(1)} fusion(f32[512,4,1024]{2,0,1:T(8,128)} %fusion.64, bf16[1024,128]{0,1:T(8,128)(2,1)} %get-tuple-element.496, f32[512,4,1024]{2,0,1:T(8,128)} %copy-done.10, f32[4,512]{1,0:T(4,128)S(1)} %get-tuple-element.458, pred[512,1024]{1,0:T(8,128)(4,1)S(1)} %compare_and_fusion.2), kind=kOutput, calls=%fused_computation.18.clone.1 | convolution fusion | flops 560204800 | bytes 18096128 | tf_op jit(solution)/shard_map/while/body/eval_jaxpr/hqk,kd->qhd/dot_general | solution.py:74
  243.7 5.8 %fusion.66 = bf16[4,512,128]{1,2,0:T(8,128)(2,1)S(1)} fusion(bf16[1024,128]{1,0:T(8,128)(2,1)S(1)} %get-tuple-element.497, f32[512,4,1024]{2,0,1:T(8,128)} %copy-done.10, f32[4,512]{1,0:T(4,128)S(1)} %get-tuple-element.458, pred[512,1024]{1,0:T(8,128)(4,1)S(1)} %compare_and_fusion.2), kind=kOutput, calls=%fused_computation.17.clone.1 | convolution fusion | flops 545521664 | bytes 9707520 | tf_op jit(solution)/shard_map/while/body/eval_jaxpr/hqk,kd->qhd/dot_general | solution.py:65
  253.1 4.5 fusion.64
  257.6 2.3 bitcast_reduce_fusion.2
  259.9 3.2 copy-done.10
  263.1 4.4 fusion.68
  267.5 16.1 %fusion.67 = f32[1024,128]{1,0:T(8,128)S(1)} fusion(bf16[512,4,128]{0,2,1:T(8,128)(2,1)S(1)} %bitcast.202, f32[512,4,1024]{2,0,1:T(8,128)} %fusion.64, f32[1024,128]{1,0:T(8,128)S(1)} %copy-done.5, pred[]{:T(512)S(6)} %compare.3, f32[512,4,1024]{2,0,1:T(8,128)} %copy-done.10, f32[4,512]{1,0:T(4,128)S(1)} %get-tuple-element.458, ...), kind=kOutput, calls=%fused_computation.21.clone.1 | convolution fusion | flops 560204800 | bytes 18882560 | tf_op jit(solution)/shard_map/while/body/eval_jaxpr/hqk,qhd->kd/dot_general | solution.py:77
  284.5 16.9 %fusion.65 = bf16[4,512,128]{1,2,0:T(8,128)(2,1)S(1)} fusion(f32[512,4,1024]{2,0,1:T(8,128)} %fusion.64, bf16[1024,128]{0,1:T(8,128)(2,1)} %get-tuple-element.496, f32[512,4,1024]{2,0,1:T(8,128)} %copy-done.10, f32[4,512]{1,0:T(4,128)S(1)} %get-tuple-element.458, pred[512,1024]{1,0:T(8,128)(4,1)S(1)} %compare_and_fusion.2), kind=kOutput, calls=%fused_computation.18.clone.1 | convolution fusion | flops 560204800 | bytes 18096128 | tf_op jit(solution)/shard_map/while/body/eval_jaxpr/hqk,kd->qhd/dot_general | solution.py:74
  301.4 5.8 %fusion.66 = bf16[4,512,128]{1,2,0:T(8,128)(2,1)S(1)} fusion(bf16[1024,128]{1,0:T(8,128)(2,1)S(1)} %get-tuple-element.497, f32[512,4,1024]{2,0,1:T(8,128)} %copy-done.10, f32[4,512]{1,0:T(4,128)S(1)} %get-tuple-element.458, pred[512,1024]{1,0:T(8,128)(4,1)S(1)} %compare_and_fusion.2), kind=kOutput, calls=%fused_computation.17.clone.1 | convolution fusion | flops 545521664 | bytes 9707520 | tf_op jit(solution)/shard_map/while/body/eval_jaxpr/hqk,kd->qhd/dot_general | solution.py:65
  308.7 11.4 %convolution_bitcast_fusion = f32[4096,512]{0,1:T(8,128)} fusion(bf16[1024,512]{0,1:T(8,128)(2,1)} %get-tuple-element.252, bf16[1024,4096]{1,0:T(8,128)(2,1)} %bitcast.8), kind=kOutput, calls=%fused_computation.38 | convolution fusion | flops 4294967296 | bytes 17825792 | tf_op jit(solution)/shard_map/dot_general | solution.py:106
  321.1 1.1 convert_bitcast_fusion
  322.7 2.2 reduce.6
  325.7 4.8 all-to-all-start.6
  330.9 2.2 reduce.5
  333.9 2.7 all-to-all-done.6
  336.6 5.6 %all-to-all-start.5 = ((bf16[8,2,8192]{2,1,0:T(2,128)(2,1)}), bf16[8,2,8192]{2,1,0:T(2,128)(2,1)}, u32[]{:S(2)}, u32[]{:S(2)}) async-start(bf16[8,2,8192]{2,1,0:T(2,128)(2,1)} %reshape.155), calls=%async_computation.5 | async-start | bytes 524288 | tf_op jit(solution)/shard_map/all_to_all | solution.py:115
  342.2 1.8 copy.126
  344.0 7.1 %reduce.4 = bf16[1024,512]{1,0:T(8,128)(2,1)S(1)} reduce(bf16[1024,1,512]{2,1,0:T(2,128)(2,1)S(1)} %bitcast.207, bf16[]{:T(256)} %broadcast.152), dimensions={1}, to_apply=%bitcast.127.reduce_sub_computation | reduce | bytes 2097154
  351.1 1.6 reshape.153
  352.7 4.8 all-to-all-start.4
  358.9 1.2 reshape.156
  361.2 10.9 %all-to-all-done.4 = bf16[8,2,32768]{2,1,0:T(2,128)(2,1)S(1)} async-done(((bf16[8,2,32768]{2,1,0:T(2,128)(2,1)}), bf16[8,2,32768]{2,1,0:T(2,128)(2,1)S(1)}, u32[]{:S(2)}, u32[]{:S(2)}) %all-to-all-start.4) | async-done | bytes 1048608 | tf_op jit(solution)/shard_map/all_to_all | solution.py:114
  374.0 1.3 copy.132
  375.3 178.6 %reduce-scatter.2.cloned.1.call-done = f32[128,512]{0,1:T(8,128)} async-done(((f32[4096,512]{0,1:T(8,128)}), f32[128,512]{0,1:T(8,128)}) %reduce-scatter.2.cloned.1.call-update) | async-done | bytes 262160 | tf_op jit(solution)/shard_map/reduce_scatter | solution.py:105
  (92 shorter events, 28.5 us)
Async XLA Ops:
  12.0 11.6 %all-to-all-start.1 = ((bf16[8,2,8192]{2,1,0:T(2,128)(2,1)}), bf16[8,2,8192]{2,1,0:T(2,128)(2,1)S(1)}, u32[]{:S(2)}, u32[]{:S(2)}) async-start(bf16[8,2,8192]{2,1,0:T(2,128)(2,1)} %reshape.149), calls=%async_computation.1 | async-start | bytes 524288 | tf_op jit(solution)/shard_map/all_to_all | solution.py:29
  23.7 33.9 %all-to-all-start.2 = ((bf16[8,2,8192]{2,1,0:T(2,128)(2,1)}), bf16[8,2,8192]{2,1,0:T(2,128)(2,1)}, u32[]{:S(2)}, u32[]{:S(2)}) async-start(bf16[8,2,8192]{2,1,0:T(2,128)(2,1)} %reshape.151), calls=%async_computation.2 | async-start | bytes 524288 | tf_op jit(solution)/shard_map/all_to_all | solution.py:30
  57.6 19.3 %all-to-all-start = ((bf16[8,2,32768]{2,1,0:T(2,128)(2,1)}), bf16[8,2,32768]{2,1,0:T(2,128)(2,1)S(1)}, u32[]{:S(2)}, u32[]{:S(2)}) async-start(bf16[8,2,32768]{2,1,0:T(2,128)(2,1)} %reshape.147), calls=%async_computation | async-start | bytes 2097152 | tf_op jit(solution)/shard_map/all_to_all | solution.py:28
  62.4 119.7 %all-gather.2.cloned.1.call-start = ((), (), s32[]{:S(2)}) async-start(), calls=%async_computation.8 | async-start | bytes 4325376 | tf_op jit(solution)/shard_map/all_gather | solution.py:24
  82.4 19.5 %copy-start.9 = (s32[1,32]{1,0:T(1,128)S(1)}, s32[1,32]{1,0:T(1,128)}, u32[]{:S(2)}) copy-start(s32[1,32]{1,0:T(1,128)} %param.13) | copy-start | bytes 388
  82.4 99.7 %all-to-all-start.3 = ((bf16[8,1,128,4096]{3,2,1,0:T(8,128)(2,1)}), bf16[8,1,128,4096]{3,2,1,0:T(8,128)(2,1)}, u32[]{:S(2)}, u32[]{:S(2)}) async-start(bf16[8,1,128,4096]{3,2,1,0:T(8,128)(2,1)} %stack.2), calls=%async_computation.3 | async-start | bytes 16777216 | tf_op jit(solution)/shard_map/all_to_all | solution.py:18
  88.8 465.1 %reduce-scatter.2.cloned.1.call-start = ((), (), s32[]{:S(2)}) async-start(), calls=%async_computation.9 | async-start | bytes 8650752 | tf_op jit(solution)/shard_map/reduce_scatter | solution.py:105
  196.6 4.5 copy-start.8
  203.3 3.2 copy-start.10
  206.6 3.3 copy-start.5
  226.0 0.8 copy-start.6
  243.7 5.8 %copy-start = (bf16[1024,512]{0,1:T(8,128)(2,1)S(1)}, bf16[1024,512]{0,1:T(8,128)(2,1)}, u32[]{:S(2)}) copy-start(bf16[1024,512]{0,1:T(8,128)(2,1)} %get-tuple-element.477) | copy-start | bytes 3145732 | tf_op jit(solution)/shard_map/while
  243.7 5.8 %copy-start.3 = (bf16[1024,512]{0,1:T(8,128)(2,1)S(1)}, bf16[1024,512]{0,1:T(8,128)(2,1)}, u32[]{:S(2)}) copy-start(bf16[1024,512]{0,1:T(8,128)(2,1)} %get-tuple-element.476) | copy-start | bytes 3145732 | tf_op jit(solution)/shard_map/while
  249.7 1.0 copy-start.1
  249.7 1.3 copy-start.4
  253.1 4.5 copy-start.8
  259.9 3.2 copy-start.10
  263.1 4.4 copy-start.5
  283.6 0.8 copy-start.6
  301.4 5.8 %copy-start = (bf16[1024,512]{0,1:T(8,128)(2,1)S(1)}, bf16[1024,512]{0,1:T(8,128)(2,1)}, u32[]{:S(2)}) copy-start(bf16[1024,512]{0,1:T(8,128)(2,1)} %get-tuple-element.477) | copy-start | bytes 3145732 | tf_op jit(solution)/shard_map/while
  301.4 5.8 %copy-start.3 = (bf16[1024,512]{0,1:T(8,128)(2,1)S(1)}, bf16[1024,512]{0,1:T(8,128)(2,1)}, u32[]{:S(2)}) copy-start(bf16[1024,512]{0,1:T(8,128)(2,1)} %get-tuple-element.476) | copy-start | bytes 3145732 | tf_op jit(solution)/shard_map/while
  307.4 1.0 copy-start.1
  307.4 1.3 copy-start.4
  320.1 1.0 copy-start.7
  320.1 22.1 %copy-start.2 = (bf16[1024,512]{0,1:T(8,128)(2,1)S(1)}, bf16[1024,512]{0,1:T(8,128)(2,1)}, u32[]{:S(2)}) copy-start(bf16[1024,512]{0,1:T(8,128)(2,1)} %get-tuple-element.249) | copy-start | bytes 3145732
  325.7 10.9 %all-to-all-start.6 = ((bf16[8,2,8192]{2,1,0:T(2,128)(2,1)}), bf16[8,2,8192]{2,1,0:T(2,128)(2,1)S(1)}, u32[]{:S(2)}, u32[]{:S(2)}) async-start(bf16[8,2,8192]{2,1,0:T(2,128)(2,1)} %reshape.157), calls=%async_computation.6 | async-start | bytes 524288 | tf_op jit(solution)/shard_map/all_to_all | solution.py:116
  336.6 16.2 %all-to-all-start.5 = ((bf16[8,2,8192]{2,1,0:T(2,128)(2,1)}), bf16[8,2,8192]{2,1,0:T(2,128)(2,1)}, u32[]{:S(2)}, u32[]{:S(2)}) async-start(bf16[8,2,8192]{2,1,0:T(2,128)(2,1)} %reshape.155), calls=%async_computation.5 | async-start | bytes 524288 | tf_op jit(solution)/shard_map/all_to_all | solution.py:115
  352.7 19.3 %all-to-all-start.4 = ((bf16[8,2,32768]{2,1,0:T(2,128)(2,1)}), bf16[8,2,32768]{2,1,0:T(2,128)(2,1)S(1)}, u32[]{:S(2)}, u32[]{:S(2)}) async-start(bf16[8,2,32768]{2,1,0:T(2,128)(2,1)} %reshape.153), calls=%async_computation.4 | async-start | bytes 2097152 | tf_op jit(solution)/shard_map/all_to_all | solution.py:114
Sparse Core Ops, SparseCore 0:
  65.8 83.9 all-gather.1
  320.3 233.5 reduce-scatter.1
